TPU v7x, 512 devices: a whole 4x8x8 slice. The times are simulated.
512 devices in a mesh: ops: 8 (over x, core), sec: 64 (over z, y).
Axes of the slice: x: 4, y: 8, z: 8, core: 2. Of those that a mesh axis runs over, the one named last changes fastest.
Arguments:
- wavefunction: bfloat16 [256, 16, 128, 128], P('sec'), may hold values from -6 to 6
- left_ops: bfloat16 [32, 256, 128, 128], P('ops', 'sec'), may hold values from -0.5 to 0.5
- right_ops: bfloat16 [32, 256, 128, 128], P('ops', 'sec'), may hold values from -0.5 to 0.5
- site_weights: float32 [32, 16], P('ops'), may hold values from -1 to 1
- right_sector: int32 [256, 16], replicated, may hold values from 0 to 255, as said below
- left_dims: int32 [256], replicated, may hold values from 32 to 128
- right_dims: int32 [256], replicated, may hold values from 32 to 128
- basis: bfloat16 [4, 256, 16, 128, 128], P(None, 'sec', None, 'ops')
Outputs:
- sigma: bfloat16 [256, 16, 128, 128], P('sec', None, 'ops')
- correlations: float32 [4], replicated
Inputs may be any that keep to these rules, and one draw needn't show every extreme that they name: For each two-site state, right_sector maps the 256 left sectors one to one onto the 256 right sectors. Right sector r lies on index r // 4 of sec and left sector a on index a // 4; the slabs of one index of sec go to every index of sec, 1 slabs to each.
All inputs are finite; a program needn't handle non-finite values.
Results may differ from a plain program's by a relative error of at most 0.0055.
Values may be sent and summed in bfloat16 or wider, within the bound.
A program may use at most 128 MiB of HBM per device.

v0:
```python
import jax
import jax.numpy as jnp
from jax import lax
from jax.sharding import PartitionSpec as P


def lookup(values_table, positions):
    flattened = values_table.reshape(-1)
    matches = positions[..., None] == jnp.arange(flattened.shape[0], dtype=jnp.int32)
    return jnp.sum(jnp.where(matches, flattened, 0), axis=-1)


def per_device(
    wavefunction, left_ops, right_ops, site_weights, right_sector, left_dims, right_dims, basis
):
    sectors, state_count, block_width, _ = wavefunction.shape
    term_count = left_ops.shape[0]
    peers = lax.axis_size("sec")
    position = lax.axis_index("sec")
    sector_total = right_sector.shape[0]
    item_count = sectors * state_count
    capacity = item_count // peers
    slot_count = peers * capacity
    target_dev = (right_sector // sectors).reshape(peers, item_count)
    devices = jnp.arange(peers, dtype=jnp.int32)
    onehot = (target_dev[:, :, None] == devices[None, None, :]).astype(jnp.int32)
    earlier = jnp.cumsum(onehot, axis=1) - onehot
    rank_all = jnp.sum(earlier * onehot, axis=2)
    my_target = lax.dynamic_index_in_dim(target_dev, position, 0, keepdims=False)
    my_rank = lax.dynamic_index_in_dim(rank_all, position, 0, keepdims=False)
    my_slot = my_target * capacity + my_rank
    slot_match = my_slot[:, None] == jnp.arange(slot_count, dtype=jnp.int32)[None, :]
    source_item = jnp.sum(
        jnp.where(slot_match, jnp.arange(item_count, dtype=jnp.int32)[:, None], 0), axis=0
    )
    slot_used = jnp.any(slot_match, axis=0)
    indices = jnp.arange(block_width, dtype=jnp.int32)
    my_sectors = lax.dynamic_slice_in_dim(right_sector, position * sectors, sectors, 0)
    my_left_dims = lax.dynamic_slice_in_dim(left_dims, position * sectors, sectors, 0)
    paired_dims = lookup(right_dims, my_sectors)
    keep_mask = (indices[None, None, :, None] < my_left_dims[:, None, None, None]) & (
        indices[None, None, None, :] < paired_dims[:, :, None, None]
    )
    masked = jnp.where(keep_mask, wavefunction, jnp.zeros_like(wavefunction))
    owned = position * sectors + jnp.arange(sectors, dtype=jnp.int32)
    matches_right = right_sector[None, :, :] == owned[:, None, None]
    anchor = jnp.sum(
        jnp.where(matches_right, jnp.arange(sector_total, dtype=jnp.int32)[None, :, None], 0),
        axis=1,
    )
    anchor_dev = anchor // sectors
    anchor_item = anchor % sectors * state_count + jnp.arange(state_count, dtype=jnp.int32)[None, :]
    anchor_rank = lookup(rank_all, anchor_dev * item_count + anchor_item)
    gather_rows = (anchor_dev * capacity + anchor_rank).reshape(-1)
    anchor_dims = lookup(left_dims, anchor)
    own_dims = lax.dynamic_slice_in_dim(right_dims, position * sectors, sectors, 0)
    out_keep = (indices[None, None, :, None] < anchor_dims[:, :, None, None]) & (
        indices[None, None, None, :] < own_dims[:, None, None, None]
    )
    products = jnp.stack(
        [
            jnp.einsum(
                "jxy,jpyz->jpxz", left_ops[term], masked, preferred_element_type=jnp.float32
            ).astype(jnp.bfloat16)
            for term in range(term_count)
        ]
    )
    flattened = products.reshape(term_count, item_count, block_width, block_width)
    outgoing = jnp.take(flattened, source_item, axis=1) * slot_used[None, :, None, None].astype(
        jnp.bfloat16
    )
    incoming = lax.all_to_all(outgoing, "sec", split_axis=1, concat_axis=1, tiled=True)
    arrived = jnp.take(incoming, gather_rows, axis=1).reshape(
        term_count, sectors, state_count, block_width, block_width
    )
    partial_value = jnp.zeros((sectors, state_count, block_width, block_width), jnp.float32)
    for term in range(term_count):
        partial_value = (
            partial_value
            + jnp.einsum(
                "jpxy,jyz->jpxz", arrived[term], right_ops[term], preferred_element_type=jnp.float32
            )
            * site_weights[term][None, :, None, None]
        )
    partial_value = jnp.where(out_keep, partial_value, 0.0)
    sigma_block = lax.psum_scatter(partial_value, "ops", scatter_dimension=2, tiled=True).astype(
        jnp.bfloat16
    )
    local_correlation = jnp.einsum(
        "vjpxy,jpxy->v", basis, sigma_block, preferred_element_type=jnp.float32
    )
    correlations = lax.psum(local_correlation, ("ops", "sec"))
    return (sigma_block, correlations)


def solution(mesh):
    in_specs = (
        P("sec", None, None, None),
        P("ops", "sec", None, None),
        P("ops", "sec", None, None),
        P("ops", None),
        P(),
        P(),
        P(),
        P(None, "sec", None, "ops", None),
    )
    out_specs = (P("sec", None, "ops", None), P())
    return jax.shard_map(
        per_device, mesh=mesh, in_specs=in_specs, out_specs=out_specs, check_vma=False
    )
```

profile of v0, /device:TPU:1, one launch (start us, length us, event | category | flops | bytes accessed | tf_op | source)
XLA Modules:
  0.0 505.0 jit_solution(2333832717340481551)
XLA Ops:
  7.2 0.0 copy-start
  7.2 0.8 add_select_fusion.1
  8.0 0.1 copy.60
  8.1 0.1 reshape.157
  8.2 0.1 copy.61
  8.3 2.3 fusion.3
  10.5 0.2 add_reduce_fusion
  10.7 0.1 select_reduce_fusion.4
  10.8 0.1 fusion.26
  11.0 0.8 constant_dynamic-slice_fusion
  11.7 0.8 dynamic_slice.17
  12.5 0.1 iota_compare_fusion.8
  12.6 0.1 copy.64
  12.6 0.9 select_reduce_fusion.1
  13.5 0.1 iota_compare_fusion.6
  13.6 0.0 copy-start.7
  13.6 0.0 copy-start.8
  13.6 2.9 convolution_convert_fusion.2
  16.6 0.0 copy-done.7
  16.6 0.0 copy-done.8
  16.6 1.2 convolution_convert_fusion.1
  17.8 1.2 convolution_convert_fusion
  19.0 1.2 convolution_convert_fusion.3
  20.3 3.8 pad_maximum_fusion
  24.1 8.9 %gather_fusion = bf16[64,4,128,128]{2,3,1,0:T(8,128)(2,1)} fusion(bf16[4,64,128,128]{2,3,1,0:T(8,128)(2,1)} %pad_maximum_fusion, s32[1024]{0:T(1024)S(1)} %pad_clamp_fusion.1), kind=kCustom, calls=%fused_computation.clone | custom fusion | bytes 16777472 | tf_op jit(solution)/shard_map/jit(_take)/gather | solution.py:69
  33.0 7.5 %bitcast_multiply_fusion = bf16[4,64,128,128]{2,3,0,1:T(8,128)(2,1)} fusion(bf16[64,4,128,128]{2,3,1,0:T(8,128)(2,1)} %gather_fusion, pred[64]{0:T(512)(128)(4,1)S(1)} %compare_and_fusion.1, bf16[64]{0:T(256)(128)(2,1)S(1)} %convert_element_type.47), kind=kLoop, calls=%fused_computation.3 | loop fusion | flops 8388608 | bytes 16777408 | tf_op jit(solution)/shard_map/mul | solution.py:69
  40.5 0.0 copy-start.5
  40.5 0.0 copy-start.3
  40.5 0.0 copy-start.6
  40.5 0.0 copy-start.4
  40.5 17.5 %all-to-all-start = ((bf16[4,64,128,128]{2,3,0,1:T(8,128)(2,1)}), bf16[4,64,128,128]{2,3,0,1:T(8,128)(2,1)}, u32[]{:S(2)}, u32[]{:S(2)}) async-start(bf16[4,64,128,128]{2,3,0,1:T(8,128)(2,1)} %bitcast_multiply_fusion), calls=%async_computation | async-start | bytes 16777216 | tf_op jit(solution)/shard_map/all_to_all | solution.py:72
  58.0 0.2 reduce-scatter.2.cloned.1.call-start
  58.3 0.0 copy-done.5
  58.3 0.1 dynamic_slice.16
  58.4 0.1 copy.62
  58.4 0.0 copy-done.3
  58.4 0.2 select_reduce_fusion.3
  58.7 0.1 reduce_sum.63
  58.7 0.1 reshape.158
  58.8 0.3 select_reduce_fusion
  59.2 0.1 reduce_sum.65
  59.3 0.0 copy-done.6
  59.3 0.2 select_reduce_fusion.2
  59.5 0.1 iota_compare_fusion.9
  59.6 0.0 copy-done.4
  59.6 0.1 iota_compare_fusion.7
  59.7 254.2 %all-to-all-done = bf16[4,64,128,128]{2,3,0,1:T(8,128)(2,1)} async-done(((bf16[4,64,128,128]{2,3,0,1:T(8,128)(2,1)}), bf16[4,64,128,128]{2,3,0,1:T(8,128)(2,1)}, u32[]{:S(2)}, u32[]{:S(2)}) %all-to-all-start) | async-done | bytes 8388640 | tf_op jit(solution)/shard_map/all_to_all | solution.py:72
  313.9 8.9 %gather_fusion.1 = bf16[64,4,128,128]{2,3,1,0:T(8,128)(2,1)} fusion(bf16[4,64,128,128]{2,3,0,1:T(8,128)(2,1)} %all-to-all-done, s32[1024]{0:T(1024)S(1)} %pad_clamp_fusion), kind=kCustom, calls=%fused_computation.1.clone | custom fusion | bytes 16777472 | tf_op jit(solution)/shard_map/jit(_take)/gather | solution.py:73
  322.8 7.5 %select_bitcast_fusion = bf16[4,64,128,128]{2,3,0,1:T(8,128)(2,1)} fusion(bf16[64,4,128,128]{2,3,1,0:T(8,128)(2,1)} %gather_fusion.1, pred[64]{0:T(512)(128)(4,1)S(1)} %get-tuple-element.3), kind=kLoop, calls=%fused_computation.4 | loop fusion | flops 4194304 | bytes 16777280 | tf_op jit(solution)/shard_map/jit(_take)/select_n | solution.py:73
  330.3 3.9 fusion.39
  334.2 0.0 copy-done.2
  334.2 0.9 fusion.8
  335.1 0.9 fusion.10
  336.0 0.9 fusion.12
  336.9 5.0 add_select_fusion
  341.9 0.0 reduce-scatter.2.cloned.1.call-update
  341.9 52.5 %reduce-scatter.2.cloned.1.call-done = f32[4,16,16,128]{3,2,1,0:T(8,128)} async-done(((f32[4,16,128,128]{3,2,1,0:T(8,128)}), f32[4,16,16,128]{3,2,1,0:T(8,128)}) %reduce-scatter.2.cloned.1.call-update) | async-done | bytes 524304 | tf_op jit(solution)/shard_map/reduce_scatter | solution.py:86
  394.4 1.1 convert_bitcast_fusion
  395.5 0.0 copy-done
  395.5 0.0 copy-start.1
  395.5 1.6 convolution_bitcast_fusion
  397.1 100.3 %psum.7 = f32[4]{0:T(128)} all-reduce(f32[4]{0:T(128)S(1)} %convolution_bitcast_fusion), channel_id=1, replica_groups=mesh['ops'=8,'sec'=64] {'ops','sec'}, use_global_device_ids=true, to_apply=%region_9.11 | all-reduce | flops 4 | bytes 32 | tf_op jit(solution)/shard_map/psum | solution.py:92
  497.4 0.0 copy-done.1
  497.4 0.7 convert_element_type.48
  (10 shorter events, 0.1 us)
Async XLA Ops:
  7.2 388.3 %copy-start = (bf16[4,4,16,16,128]{4,3,2,1,0:T(8,128)(2,1)S(1)}, bf16[4,4,16,16,128]{4,3,2,1,0:T(8,128)(2,1)}, u32[]{:S(2)}) copy-start(bf16[4,4,16,16,128]{4,3,2,1,0:T(8,128)(2,1)} %param.17) | copy-start | bytes 3145732
  13.6 3.0 copy-start.7
  13.6 3.0 copy-start.8
  40.5 17.8 %copy-start.5 = (s32[256]{0:T(256)S(1)}, s32[256]{0:T(256)}, u32[]{:S(2)}) copy-start(s32[256]{0:T(256)} %param.16) | copy-start | bytes 3076
  40.5 18.0 %copy-start.3 = (s32[256,16]{0,1:T(8,128)S(1)}, s32[256,16]{0,1:T(8,128)}, u32[]{:S(2)}) copy-start(s32[256,16]{0,1:T(8,128)} %param.14) | copy-start | bytes 49156
  40.5 18.8 %copy-start.6 = (s32[256]{0:T(256)S(1)}, s32[256]{0:T(256)}, u32[]{:S(2)}) copy-start(s32[256]{0:T(256)} %param.15) | copy-start | bytes 3076
  40.5 19.1 %copy-start.4 = (f32[4,16]{1,0:T(4,128)S(1)}, f32[4,16]{1,0:T(4,128)}, u32[]{:S(2)}) copy-start(f32[4,16]{1,0:T(4,128)} %param.13) | copy-start | bytes 772
  40.5 273.4 %all-to-all-start = ((bf16[4,64,128,128]{2,3,0,1:T(8,128)(2,1)}), bf16[4,64,128,128]{2,3,0,1:T(8,128)(2,1)}, u32[]{:S(2)}, u32[]{:S(2)}) async-start(bf16[4,64,128,128]{2,3,0,1:T(8,128)(2,1)} %bitcast_multiply_fusion), calls=%async_computation | async-start | bytes 16777216 | tf_op jit(solution)/shard_map/all_to_all | solution.py:72
  58.0 336.4 %reduce-scatter.2.cloned.1.call-start = ((), (), s32[]{:S(2)}) async-start(), calls=%async_computation.2 | async-start | bytes 4718592 | tf_op jit(solution)/shard_map/reduce_scatter | solution.py:86
  330.3 4.0 copy-start.2
  395.5 102.0 %copy-start.1 = (f32[4,16,16,128]{3,2,1,0:T(8,128)S(1)}, f32[4,16,16,128]{3,2,1,0:T(8,128)}, u32[]{:S(2)}) copy-start(f32[4,16,16,128]{3,2,1,0:T(8,128)} %reduce-scatter.2.cloned.1.call-done) | copy-start | bytes 1572868
Sparse Core Ops, SparseCore 0:
  342.1 52.2 reduce-scatter.1
where the time goes:
time: 506 us; the launch traced here: 505 us
  waiting for transfers between devices  307 us (61%)
  blocking collectives  100 us (20%)
  other arithmetic  26 us (5%)
  local copies, waits for them, and re-layouts  24.1 us (5%)
  starting transfers between devices  17.8 us (4%)
  matrix products  15.9 us (3%)
  between operations  14.3 us (3%)
    all_to_all x1, waiting for transfers between devices, per_device(): lax.all_to_all(outgoing, 'sec', split_axis=1, concat_axis=1, tiled=True)  254 us
    psum x1, blocking collectives, per_device(): correlations = lax.psum(local_correlation, ('ops', 'sec'))  100 us
    reduce_scatter x1, waiting for transfers between devices, per_device(): lax.psum_scatter(partial_value, 'ops', scatter_dimension=2, tiled=True)  52.5 us
    all_to_all x1, starting transfers between devices, per_device(): lax.all_to_all(outgoing, 'sec', split_axis=1, concat_axis=1, tiled=True)  17.5 us
  transfers between devices with their start and end apart: 2, of which 2 were waited for; matrix products, arithmetic and copies ran while one was open for 0% of the time, Pallas kernels for 0%

commit v1 on v0

v1 whole, which is shorter than its diff:
```python
import jax
import jax.numpy as jnp
from jax import lax
from jax.experimental import pallas as pl
from jax.experimental.pallas import tpu as pltpu
from jax.sharding import Mesh
from jax.sharding import PartitionSpec as P


def contract_kernel(index_ref, weight_ref, slab_ref, left_ref, right_ref, out_ref):
    width = slab_ref.shape[-1]
    terms = left_ref.shape[1]
    peers_y = left_ref.shape[0]
    rows = lax.broadcasted_iota(jnp.int32, (width, width), 0)
    columns = lax.broadcasted_iota(jnp.int32, (width, width), 1)

    def edge(position, carry):
        z_from = position // peers_y
        y_from = position % peers_y
        left_at = index_ref[0, position]
        right_at = index_ref[1, position]
        keep = (rows < index_ref[2, position]) & (columns < index_ref[3, position])
        slab = jnp.where(keep, slab_ref[position].astype(jnp.float32), 0.0).astype(jnp.bfloat16)
        total = jnp.zeros((width, width), jnp.float32)
        for term in range(terms):
            product = jnp.dot(
                left_ref[y_from, term, left_at], slab, preferred_element_type=jnp.float32
            )
            summand = jnp.dot(
                product.astype(jnp.bfloat16),
                right_ref[z_from, term, right_at],
                preferred_element_type=jnp.float32,
            )
            total += summand * weight_ref[term, position]
        out_ref[position] = jnp.where(keep, total, 0.0)
        return carry

    lax.fori_loop(0, slab_ref.shape[0], edge, 0)


def contract(index_table, weight_table, slabs, left_all, right_all):
    smem = pl.BlockSpec(memory_space=pltpu.SMEM)
    vmem = pl.BlockSpec(memory_space=pltpu.VMEM)
    return pl.pallas_call(
        contract_kernel,
        out_shape=jax.ShapeDtypeStruct(slabs.shape, jnp.float32),
        in_specs=[smem, smem, vmem, vmem, vmem],
        out_specs=vmem,
    )(index_table, weight_table, slabs, left_all, right_all)


def per_device(
    wavefunction, left_ops, right_ops, site_weights, right_sector, left_dims, right_dims, basis
):
    sectors, states, width, _ = wavefunction.shape
    terms = left_ops.shape[0]
    size_z, size_y = lax.axis_size("z"), lax.axis_size("y")
    groups = size_z * size_y
    items = sectors * states
    me_z, me_y, me_o = lax.axis_index("z"), lax.axis_index("y"), lax.axis_index("ops")
    right_groups = right_sector.reshape(groups, items)
    row_groups = lax.dynamic_slice_in_dim(right_groups, me_z * size_y, size_y, 0)
    wanted = jnp.arange(size_z, dtype=jnp.int32) * size_y + me_y
    match = (row_groups // sectors)[None, :, :] == wanted[:, None, None]
    item_at = jnp.arange(items, dtype=jnp.int32)
    item = jnp.sum(jnp.where(match, item_at, 0), axis=2)
    right_at = jnp.sum(jnp.where(match, row_groups[None], 0), axis=2)
    source = (me_z * size_y + jnp.arange(size_y, dtype=jnp.int32)) * sectors
    left_at = source[None, :] + item // states
    sector_at = jnp.arange(groups * sectors, dtype=jnp.int32)
    left_dim = jnp.sum(jnp.where(left_at[..., None] == sector_at, left_dims, 0), axis=-1)
    right_dim = jnp.sum(jnp.where(right_at[..., None] == sector_at, right_dims, 0), axis=-1)
    index_table = jnp.stack(
        [
            (item // states).reshape(-1),
            (right_at % sectors).reshape(-1),
            left_dim.reshape(-1),
            right_dim.reshape(-1),
        ]
    )
    state = (item % states).reshape(-1)
    state_at = jnp.arange(states, dtype=jnp.int32)
    weight_table = jnp.sum(
        jnp.where(state[None, :, None] == state_at, site_weights[:, None, :], 0.0), axis=-1
    )
    my_groups = lax.dynamic_index_in_dim(right_groups, me_z * size_y + me_y, 0, keepdims=False)
    targets = me_o * size_y + jnp.arange(size_y, dtype=jnp.int32)
    chosen = jnp.sum(
        jnp.where((my_groups // sectors)[None, :] == targets[:, None], item_at, 0), axis=1
    )
    outgoing = jnp.take(wavefunction.reshape(items, width, width), chosen, axis=0)
    arrived = lax.all_to_all(outgoing, "y", split_axis=0, concat_axis=0, tiled=True)
    slabs = lax.all_gather(arrived, "ops", axis=0, tiled=True)
    left_all = lax.all_gather(left_ops, "y", axis=0)
    right_all = lax.all_gather(right_ops, "z", axis=0)
    partial = contract(index_table, weight_table, slabs, left_all, right_all)
    summed = lax.psum_scatter(partial, "ops", scatter_dimension=1, tiled=True).astype(jnp.bfloat16)
    received = lax.all_to_all(summed, "z", split_axis=0, concat_axis=0, tiled=True)
    owned = (me_z * size_y + me_y) * sectors + jnp.arange(sectors, dtype=jnp.int32)
    slot = jnp.sum(
        jnp.where(right_sector[None] == owned[:, None, None], sector_at[None, :, None] // sectors, 0),
        axis=1,
    )
    sigma = jnp.take(received, slot.reshape(-1), axis=0).reshape(sectors, states, -1, width)
    local = jnp.einsum("vjpxy,jpxy->v", basis, sigma, preferred_element_type=jnp.float32)
    return sigma, lax.psum(local, ("ops", "z", "y"))


def solution(mesh):
    grid = Mesh(mesh.devices.reshape(8, 8, 8), ("ops", "z", "y"))
    sec = ("z", "y")
    in_specs = (
        P(sec, None, None, None),
        P("ops", sec, None, None),
        P("ops", sec, None, None),
        P("ops", None),
        P(),
        P(),
        P(),
        P(None, sec, None, "ops", None),
    )
    out_specs = (P(sec, None, "ops", None), P())
    return jax.shard_map(
        per_device, mesh=grid, in_specs=in_specs, out_specs=out_specs, check_vma=False
    )
```

time: 506 us -> 374 us (0.74)
  waiting for transfers between devices: 307 us -> 194 us
  Pallas kernels: 0 us -> 27 us
  local copies, waits for them, and re-layouts: 24.1 us -> 3.66 us
  other arithmetic: 26 us -> 7.68 us
  blocking collectives: 100 us -> 117 us
  matrix products: 15.9 us -> 2.9 us
  starting transfers between devices: 17.8 us -> 6.62 us
    all_to_all x1, waiting for transfers between devices: 254 us -> 9.44 us  [per_device(): lax.all_to_all(summed, 'z', split_axis=0, concat_axis=0, tiled=True)]
    all_gather x0 -> x3, waiting for transfers between devices: none -> 145 us  [the longest x1 59.4 us: per_device(): right_all = lax.all_gather(right_ops, 'z', axis=0)]
    pallas_call x0 -> x1, Pallas kernels: none -> 27 us  [contract(): pl.pallas_call(contract_kernel, out_shape=jax.ShapeDtypeStruct(slabs.shap...]
    all_to_all x0 -> x1, blocking collectives: none -> 17 us  [per_device(): lax.all_to_all(outgoing, 'y', split_axis=0, concat_axis=0, tiled=True)]
    gather x2, local copies, waits for them, and re-layouts: 17.8 us -> 1.23 us  [the longest x1 0.63 us: per_device(): jnp.take(received, slot.reshape(-1), axis=0)]
    reduce_scatter x1, waiting for transfers between devices: 52.5 us -> 38.2 us  [per_device(): lax.psum_scatter(partial, 'ops', scatter_dimension=1, tiled=True)]
    dot_general x9 -> x1, matrix products: 15.9 us -> 2.9 us  [per_device(): jnp.einsum('vjpxy,jpxy->v', basis, sigma, preferred_element_type=jnp.floa...]
    all_to_all x1, starting transfers between devices: 17.5 us -> 6.46 us  [per_device(): lax.all_to_all(summed, 'z', split_axis=0, concat_axis=0, tiled=True)]
  transfers between devices with their start and end apart: 2 -> 5, of which waited for: 2 -> 5; matrix products, arithmetic and copies ran while one was open for 0% -> 1% of each run, Pallas kernels for 0% -> 0%
where the time goes in v1:
time: 374 us
  waiting for transfers between devices  194 us (52%)
  blocking collectives  117 us (31%)
  Pallas kernels  27 us (7%)
  between operations  13.9 us (4%)
  other arithmetic  7.68 us (2%)
  starting transfers between devices  6.62 us (2%)
    psum x1, blocking collectives, per_device(): return (sigma, lax.psum(local, ('ops', 'z', 'y')))  100 us
    all_gather x1, waiting for transfers between devices, per_device(): right_all = lax.all_gather(right_ops, 'z', axis=0)  59.4 us
    all_gather x1, waiting for transfers between devices, per_device(): left_all = lax.all_gather(left_ops, 'y', axis=0)  59.2 us
    reduce_scatter x1, waiting for transfers between devices, per_device(): lax.psum_scatter(partial, 'ops', scatter_dimension=1, tiled=True)  38.2 us
    pallas_call x1, Pallas kernels, contract(): pl.pallas_call(contract_kernel, out_shape=jax.ShapeDtypeStruct(slabs.shap...  27 us
    all_gather x1, waiting for transfers between devices, per_device(): slabs = lax.all_gather(arrived, 'ops', axis=0, tiled=True)  26.8 us
    all_to_all x1, blocking collectives, per_device(): lax.all_to_all(outgoing, 'y', split_axis=0, concat_axis=0, tiled=True)  17 us
    all_to_all x1, waiting for transfers between devices, per_device(): lax.all_to_all(summed, 'z', split_axis=0, concat_axis=0, tiled=True)  9.44 us
  transfers between devices with their start and end apart: 5, of which 5 were waited for; matrix products, arithmetic and copies ran while one was open for 1% of the time, Pallas kernels for 0%

profile of v1, /device:TPU:1, one launch (start us, length us, event | category | flops | bytes accessed | tf_op | source)
XLA Modules:
  0.0 373.7 jit_solution(12140930807120601851)
XLA Ops:
  7.2 0.0 copy-start
  7.2 0.0 all-gather.6.cloned.1.call-start
  7.2 1.0 copy.16
  8.2 0.1 reshape.324
  8.3 0.2 select_reduce_fusion.4
  8.5 0.2 copy-done
  8.8 0.6 gather_fusion
  9.4 0.1 broadcast_select_fusion
  9.5 17.0 %all_to_all.10 = bf16[8,128,128]{2,1,0:T(8,128)(2,1)} all-to-all(bf16[8,128,128]{2,1,0:T(8,128)(2,1)S(1)} %broadcast_select_fusion), channel_id=1, replica_groups=mesh['ops'=8,'z'=8,'y'=8] {'y'}, dimensions={0} | all-to-all | bytes 524288 | tf_op jit(solution)/shard_map/all_to_all | solution.py:92
  26.5 0.0 all-gather.6.cloned.1.call-update
  26.5 0.0 all-gather.8.cloned.1.call-start
  26.5 0.7 all-gather.8.cloned.1.call-update
  27.3 0.0 all-gather.10.cloned.1.call-start
  27.3 0.7 all-gather.10.cloned.1.call-update
  28.0 0.0 reduce-scatter.2.cloned.1.call-start
  28.1 0.4 fusion.2
  28.5 0.1 reduce_sum.73
  28.6 0.1 reduce_sum.78
  28.6 0.1 reduce_sum.75
  28.8 1.0 select_reduce_fusion.1
  29.7 0.1 stack_reshape.8
  29.8 1.0 select_reduce_fusion
  30.8 0.1 stack_reshape.9
  30.9 0.6 pad_add_fusion.index_ref
  31.5 1.4 select_reduce_fusion.3.weight_ref
  32.8 26.8 %all-gather.6.cloned.1.call-done.slab_ref = bf16[64,128,128]{2,1,0:T(8,128)(2,1)} async-done(((bf16[8,128,128]{2,1,0:T(8,128)(2,1)}), bf16[64,128,128]{2,1,0:T(8,128)(2,1)}) %all-gather.6.cloned.1.call-update) | async-done | bytes 2097168 | tf_op jit(solution)/shard_map/all_gather | solution.py:93
  59.7 59.2 %all-gather.8.cloned.1.call-done = bf16[32,4,128,128]{3,2,1,0:T(8,128)(2,1)} async-done(((bf16[4,4,128,128]{3,2,1,0:T(8,128)(2,1)}), bf16[32,4,128,128]{3,2,1,0:T(8,128)(2,1)}) %all-gather.8.cloned.1.call-update) | async-done | bytes 4194320 | tf_op jit(solution)/shard_map/all_gather | solution.py:94
  118.9 59.4 %all-gather.10.cloned.1.call-done = bf16[32,4,128,128]{3,2,1,0:T(8,128)(2,1)} async-done(((bf16[4,4,128,128]{3,2,1,0:T(8,128)(2,1)}), bf16[32,4,128,128]{3,2,1,0:T(8,128)(2,1)}) %all-gather.10.cloned.1.call-update) | async-done | bytes 4194320 | tf_op jit(solution)/shard_map/all_gather | solution.py:95
  178.3 27.0 %shard_map.95 = f32[64,128,128]{2,1,0:T(8,128)} custom-call(s32[4,64]{1,0:T(4,128)} %pad_add_fusion.index_ref, f32[4,64]{1,0:T(4,128)} %select_reduce_fusion.3.weight_ref, bf16[64,128,128]{2,1,0:T(8,128)(2,1)} %all-gather.6.cloned.1.call-done.slab_ref, bf16[8,4,4,128,128]{4,3,2,1,0:T(8,128)(2,1)} %bitcast.19, bf16[8,4,4,128,128]{4,3,2,1,0:T(8,128)(2,1)} %bitcast.20), custom_call_target="tpu_custom_call" | custom-call | tf_op jit(solution)/shard_map/pallas_call | solution.py:44
  205.3 0.0 copy-start.1
  205.3 0.0 reduce-scatter.2.cloned.1.call-update
  205.3 0.7 copy-done.1
  206.0 0.2 select_reduce_fusion.2
  206.2 0.1 reshape.326
  206.3 38.2 %reduce-scatter.2.cloned.1.call-done = f32[64,16,128]{2,1,0:T(8,128)} async-done(((f32[64,128,128]{2,1,0:T(8,128)}), f32[64,16,128]{2,1,0:T(8,128)}) %reduce-scatter.2.cloned.1.call-update) | async-done | bytes 524304 | tf_op jit(solution)/shard_map/reduce_scatter | solution.py:97
  244.5 1.8 convert_element_type.3
  246.3 6.5 %all-to-all-start.1 = ((bf16[64,16,128]{2,1,0:T(8,128)(2,1)}), bf16[64,16,128]{2,1,0:T(8,128)(2,1)S(1)}, u32[]{:S(2)}, u32[]{:S(2)}) async-start(bf16[64,16,128]{2,1,0:T(8,128)(2,1)} %convert_element_type.3), calls=%async_computation.2 | async-start | bytes 524288 | tf_op jit(solution)/shard_map/all_to_all | solution.py:98
  252.8 9.4 %all-to-all-done.1 = bf16[64,16,128]{2,1,0:T(8,128)(2,1)S(1)} async-done(((bf16[64,16,128]{2,1,0:T(8,128)(2,1)}), bf16[64,16,128]{2,1,0:T(8,128)(2,1)S(1)}, u32[]{:S(2)}, u32[]{:S(2)}) %all-to-all-start.1) | async-done | bytes 262176 | tf_op jit(solution)/shard_map/all_to_all | solution.py:98
  262.2 0.6 gather_fusion.1
  262.9 0.1 fusion.14
  263.0 2.9 convolution_bitcast_fusion
  265.9 0.9 broadcast_select_fusion.1
  266.8 100.4 %psum.7 = f32[4]{0:T(128)} all-reduce(f32[4]{0:T(128)S(1)} %convolution_bitcast_fusion), channel_id=1, replica_groups=mesh['ops'=8,'z'=8,'y'=8] {'ops','z','y'}, use_global_device_ids=true, to_apply=%region_8.9 | all-reduce | flops 4 | bytes 32 | tf_op jit(solution)/shard_map/psum | solution.py:106
  (17 shorter events, 0.1 us)
Async XLA Ops:
  7.2 1.6 copy-start
  7.2 52.5 %all-gather.6.cloned.1.call-start = ((), (), s32[]{:S(2)}) async-start(), calls=%async_computation.3 | async-start | bytes 2359296 | tf_op jit(solution)/shard_map/all_gather | solution.py:93
  26.5 92.4 %all-gather.8.cloned.1.call-start = ((), (), s32[]{:S(2)}) async-start(), calls=%async_computation.5 | async-start | bytes 4718592 | tf_op jit(solution)/shard_map/all_gather | solution.py:94
  27.3 151.0 %all-gather.10.cloned.1.call-start = ((), (), s32[]{:S(2)}) async-start(), calls=%async_computation.6 | async-start | bytes 4718592 | tf_op jit(solution)/shard_map/all_gather | solution.py:95
  28.0 216.5 %reduce-scatter.2.cloned.1.call-start = ((), (), s32[]{:S(2)}) async-start(), calls=%async_computation.4 | async-start | bytes 4718592 | tf_op jit(solution)/shard_map/reduce_scatter | solution.py:97
  205.3 0.7 copy-start.1
  246.3 15.9 %all-to-all-start.1 = ((bf16[64,16,128]{2,1,0:T(8,128)(2,1)}), bf16[64,16,128]{2,1,0:T(8,128)(2,1)S(1)}, u32[]{:S(2)}, u32[]{:S(2)}) async-start(bf16[64,16,128]{2,1,0:T(8,128)(2,1)} %convert_element_type.3), calls=%async_computation.2 | async-start | bytes 524288 | tf_op jit(solution)/shard_map/all_to_all | solution.py:98
Sparse Core Ops, SparseCore 0:
  26.6 32.9 all-gather.5
  61.7 57.0 all-gather.7
  120.9 57.2 all-gather.9
  205.4 39.0 reduce-scatter.1

commit v2 on v1

v2 whole, which is shorter than its diff:
```python
import jax
import jax.numpy as jnp
from jax import lax
from jax.experimental import pallas as pl
from jax.experimental.pallas import tpu as pltpu
from jax.sharding import Mesh
from jax.sharding import PartitionSpec as P

MESH = pl.DeviceIdType.MESH
RING = 8
CHIPS = 4
DISTANCE = (0, 1, 7, 2, 6, 3, 5, 4)
RANK = tuple(DISTANCE.index(d) for d in range(RING))
READY = (1, 3, 5, 7, 8)


def pair_order():
    order, before = [], 0
    for ready in READY:
        for z_rank in range(ready):
            for y_rank in range(ready):
                if max(z_rank, y_rank) >= before:
                    order.append((z_rank, y_rank))
        before = ready
    return order


ORDER = pair_order()
BOUNDS = (0,) + tuple(ready * ready for ready in READY)


def kernel(
    index_ref,
    weight_ref,
    slot_ref,
    outgoing_ref,
    left_ref,
    right_ref,
    basis_ref,
    sigma_ref,
    sums_ref,
    slab_ref,
    left_land,
    right_land,
    left_all,
    right_all,
    split_ref,
    pair_ref,
    row_ref,
    chip_ref,
    final_ref,
    arrive_ref,
    tally_ref,
    local_sem,
    slab_send,
    slab_recv,
    spread_send,
    spread_recv,
    mate_send,
    mate_recv,
    ring_send,
    ring_recv,
    pair_send,
    pair_recv,
    chip_send,
    chip_recv,
    final_send,
    final_recv,
    tally_send,
    tally_recv,
):
    me_o, me_z, me_y = lax.axis_index("ops"), lax.axis_index("z"), lax.axis_index("y")
    me_x, core = me_o // 2, me_o % 2
    mate = me_x * 2 + 1 - core
    mine = {"ops": me_o, "z": me_z, "y": me_y}
    terms, width = left_ref.shape[0], left_ref.shape[-1]
    half = terms // 2
    started = []

    def device(axis, position):
        return tuple(
            position if name == axis else mine[name] for name in ("ops", "z", "y")
        )

    def send(source, target, send_sem, recv_sem, axis, position):
        copy = pltpu.make_async_remote_copy(
            src_ref=source,
            dst_ref=target,
            send_sem=send_sem,
            recv_sem=recv_sem,
            device_id=device(axis, position),
            device_id_type=MESH,
        )
        copy.start()
        started.append(copy)
        return copy

    def chip_at(step):
        return lax.rem(me_x + step, CHIPS)

    def ring_at(position, step):
        return lax.rem(position + step, RING)

    barrier = pltpu.get_barrier_semaphore()
    for axis in ("ops", "z", "y"):
        for step in range(1, RING):
            pl.semaphore_signal(
                barrier,
                inc=1,
                device_id=device(axis, ring_at(mine[axis], step)),
                device_id_type=MESH,
            )
    pl.semaphore_wait(barrier, 3 * (RING - 1))

    own = pltpu.make_async_copy(
        outgoing_ref.at[me_y], slab_ref.at[me_o, me_y], local_sem
    )
    own.start()
    slab_copies = [
        send(
            outgoing_ref.at[ring_at(me_y, step)],
            slab_ref.at[me_o, me_y],
            slab_send.at[step],
            slab_recv.at[step],
            "y",
            ring_at(me_y, step),
        )
        for step in range(1, RING)
    ]

    sides = ((left_ref, left_land, "y"), (right_ref, right_land, "z"))
    flying = {}

    def pass_on(stage, part):
        for side, (held, land, axis) in enumerate(sides):
            for way in range(2):
                if stage == 3 and part != way:
                    continue
                here = stage if way == 0 else (RING - stage) % RING
                there = stage + 1 if way == 0 else RING - 1 - stage
                terms_at = pl.ds(part * half, half)
                source = held.at[terms_at] if stage == 0 else land.at[RANK[here], terms_at]
                sem = ((side * 2 + way) * 4 + stage) * 2 + part
                flying[side, way, stage, part] = send(
                    source,
                    land.at[RANK[there], terms_at],
                    ring_send.at[sem],
                    ring_recv.at[sem],
                    axis,
                    ring_at(mine[axis], 1 if way == 0 else RING - 1),
                )

    def take_in(stage, part):
        for side in range(2):
            for way in range(2):
                if stage == 3 and part != way:
                    continue
                flying[side, way, stage, part].wait_recv()

    def keep_block(held, kept, rank):
        def one(term, carry):
            kept[rank, term] = held[term]
            return carry

        lax.fori_loop(0, terms, one, 0)

    rows = lax.broadcasted_iota(jnp.int32, (width, width), 0)
    columns = lax.broadcasted_iota(jnp.int32, (width, width), 1)
    share = width // RING

    def contract(stage):
        def one(position, carry):
            slab = slab_ref[index_ref[0, position], index_ref[1, position]]
            z_rank, y_rank = index_ref[2, position], index_ref[3, position]
            left_at, right_at = index_ref[4, position], index_ref[5, position]
            keep = (rows < index_ref[6, position]) & (columns < index_ref[7, position])
            total = jnp.zeros((width, width), jnp.float32)
            for term in range(terms):
                product = jnp.dot(
                    left_all[y_rank, term, left_at], slab, preferred_element_type=jnp.float32
                )
                summand = jnp.dot(
                    product.astype(jnp.bfloat16),
                    right_all[z_rank, term, right_at],
                    preferred_element_type=jnp.float32,
                )
                total += summand * weight_ref[term, position]
            total = jnp.where(keep, total, 0.0)
            for owner in range(RING):
                split_ref[owner % 2, owner // 2, position] = total[
                    owner * share : (owner + 1) * share
                ]
            return carry

        lax.fori_loop(BOUNDS[stage], BOUNDS[stage + 1], one, 0)

    pair_copies, chip_copies = {}, {}

    def span(stage):
        return pl.ds(BOUNDS[stage], BOUNDS[stage + 1] - BOUNDS[stage])

    def to_mate(stage):
        pair_copies[stage] = send(
            split_ref.at[1 - core, :, span(stage)],
            pair_ref.at[:, span(stage)],
            pair_send.at[stage],
            pair_recv.at[stage],
            "ops",
            mate,
        )

    def to_chips(stage):
        pair_copies[stage].wait_recv()

        def one(position, carry):
            for chip in range(CHIPS):
                row_ref[chip, position] = (
                    split_ref[core, chip, position] + pair_ref[chip, position]
                )
            return carry

        lax.fori_loop(BOUNDS[stage], BOUNDS[stage + 1], one, 0)
        for step in range(1, CHIPS):
            chip_copies[stage, step] = send(
                row_ref.at[chip_at(step), span(stage)],
                chip_ref.at[step - 1, span(stage)],
                chip_send.at[stage * CHIPS + step],
                chip_recv.at[stage * CHIPS + step],
                "ops",
                chip_at(step) * 2 + core,
            )

    pass_on(0, 0)
    pass_on(0, 1)
    own.wait()
    for copy in slab_copies:
        copy.wait_recv()
    spread = [
        send(
            slab_ref.at[me_o],
            slab_ref.at[me_o],
            spread_send.at[step],
            spread_recv.at[step],
            "ops",
            chip_at(step) * 2 + core,
        )
        for step in range(1, CHIPS)
    ]
    mates = [
        send(slab_ref.at[me_o], slab_ref.at[me_o], mate_send.at[0], mate_recv.at[0], "ops", mate)
    ]
    keep_block(left_ref, left_all, 0)
    keep_block(right_ref, right_all, 0)
    take_in(0, 0)
    pass_on(1, 0)
    for step in range(1, CHIPS):
        spread[step - 1].wait_recv()
        block = chip_at(CHIPS - step) * 2 + core
        mates.append(
            send(
                slab_ref.at[block],
                slab_ref.at[block],
                mate_send.at[step],
                mate_recv.at[step],
                "ops",
                mate,
            )
        )
    take_in(0, 1)
    pass_on(1, 1)
    for copy in mates:
        copy.wait_recv()

    contract(0)
    to_mate(0)
    for stage in range(1, 5):
        if stage > 1:
            for part in range(2):
                take_in(stage - 1, part)
                if stage < 4:
                    pass_on(stage, part)
        for rank in range(READY[stage - 1], READY[stage]):
            keep_block(left_land.at[rank], left_all, rank)
            keep_block(right_land.at[rank], right_all, rank)
        to_chips(stage - 1)
        contract(stage)
        to_mate(stage)
    to_chips(4)
    for stage in range(5):
        for step in range(1, CHIPS):
            chip_copies[stage, step].wait_recv()

    final_copies = []
    for z_rank in reversed(range(RING)):
        for y_rank in range(RING):
            position = ORDER.index((z_rank, y_rank))
            value = row_ref[me_x, position] + chip_ref[0, position]
            value = value + chip_ref[1, position] + chip_ref[2, position]
            target = final_ref if z_rank else arrive_ref
            target[z_rank, y_rank] = value.astype(jnp.bfloat16)
        if z_rank:
            final_copies.append(
                send(
                    final_ref.at[z_rank],
                    arrive_ref.at[z_rank],
                    final_send.at[z_rank],
                    final_recv.at[z_rank],
                    "z",
                    ring_at(me_z, RING - DISTANCE[z_rank]),
                )
            )
    for copy in final_copies:
        copy.wait_recv()

    vectors = basis_ref.shape[0]

    def project(item, sums):
        value = arrive_ref[slot_ref[0, item], slot_ref[1, item]]
        sigma_ref[item] = value
        wide = value.astype(jnp.float32)
        return tuple(
            sums[vector] + basis_ref[vector, item].astype(jnp.float32) * wide
            for vector in range(vectors)
        )

    zero = jnp.zeros((share, width), jnp.float32)
    sums = lax.fori_loop(0, basis_ref.shape[1], project, (zero,) * vectors)
    now = jnp.concatenate([jnp.sum(value, axis=0, keepdims=True) for value in sums] * 2, axis=0)

    for phase, axis in enumerate(("ops", "z", "y")):
        tally_ref[phase, mine[axis]] = now
        copies = [
            send(
                tally_ref.at[phase, mine[axis]],
                tally_ref.at[phase, mine[axis]],
                tally_send.at[phase * RING + step],
                tally_recv.at[phase * RING + step],
                axis,
                ring_at(mine[axis], step),
            )
            for step in range(1, RING)
        ]
        for copy in copies:
            copy.wait_recv()
        now = tally_ref[phase, 0]
        for other in range(1, RING):
            now = now + tally_ref[phase, other]
    sums_ref[...] = now
    for copy in started:
        copy.wait_send()


def fused(index_table, weight_table, slot_table, outgoing, left_ops, right_ops, basis):
    smem = pl.BlockSpec(memory_space=pltpu.SMEM)
    vmem = pl.BlockSpec(memory_space=pltpu.VMEM)
    terms, sectors, width, _ = left_ops.shape
    pairs = RING * RING
    share = width // RING
    block = (RING, terms, sectors, width, width)
    dma = pltpu.SemaphoreType.DMA
    return pl.pallas_call(
        kernel,
        out_shape=(
            jax.ShapeDtypeStruct((pairs, share, width), jnp.bfloat16),
            jax.ShapeDtypeStruct((2 * basis.shape[0], width), jnp.float32),
        ),
        in_specs=[smem] * 3 + [vmem] * 4,
        out_specs=(vmem, vmem),
        scratch_shapes=[
            pltpu.VMEM((RING, RING, width, width), jnp.bfloat16),
            pltpu.VMEM(block, jnp.bfloat16),
            pltpu.VMEM(block, jnp.bfloat16),
            pltpu.VMEM(block, jnp.bfloat16),
            pltpu.VMEM(block, jnp.bfloat16),
            pltpu.VMEM((2, CHIPS, pairs, share, width), jnp.float32),
            pltpu.VMEM((CHIPS, pairs, share, width), jnp.float32),
            pltpu.VMEM((CHIPS, pairs, share, width), jnp.float32),
            pltpu.VMEM((CHIPS - 1, pairs, share, width), jnp.float32),
            pltpu.VMEM((RING, RING, share, width), jnp.bfloat16),
            pltpu.VMEM((RING, RING, share, width), jnp.bfloat16),
            pltpu.VMEM((3, RING, 2 * basis.shape[0], width), jnp.float32),
            dma,
            dma((RING,)),
            dma((RING,)),
            dma((CHIPS,)),
            dma((CHIPS,)),
            dma((CHIPS,)),
            dma((CHIPS,)),
            dma((32,)),
            dma((32,)),
            dma((5,)),
            dma((5,)),
            dma((5 * CHIPS,)),
            dma((5 * CHIPS,)),
            dma((RING,)),
            dma((RING,)),
            dma((3 * RING,)),
            dma((3 * RING,)),
        ],
        compiler_params=pltpu.CompilerParams(
            collective_id=0, has_side_effects=True, vmem_limit_bytes=48 << 20
        ),
    )(index_table, weight_table, slot_table, outgoing, left_ops, right_ops, basis)


def pick(table, positions):
    places = jnp.arange(table.shape[0], dtype=jnp.int32)
    return jnp.sum(jnp.where(positions[..., None] == places, table, 0), axis=-1)


def per_device(
    wavefunction, left_ops, right_ops, site_weights, right_sector, left_dims, right_dims, basis
):
    sectors, states, width, _ = wavefunction.shape
    groups = RING * RING
    items = sectors * states
    me_z, me_y, me_o = lax.axis_index("z"), lax.axis_index("y"), lax.axis_index("ops")
    right_groups = right_sector.reshape(groups, items)
    item_at = jnp.arange(items, dtype=jnp.int32)
    z_rank = jnp.array([pair[0] for pair in ORDER], jnp.int32)
    y_rank = jnp.array([pair[1] for pair in ORDER], jnp.int32)
    rank = jnp.array(RANK, jnp.int32)
    z_to = (me_z - jnp.array([DISTANCE[pair[0]] for pair in ORDER], jnp.int32)) % RING
    y_from = (me_y - jnp.array([DISTANCE[pair[1]] for pair in ORDER], jnp.int32)) % RING
    row_groups = lax.dynamic_slice_in_dim(right_groups, me_z * RING, RING, 0)
    match_from = y_from[:, None, None] == jnp.arange(RING, dtype=jnp.int32)[None, :, None]
    match = match_from & ((row_groups // sectors)[None] == (z_to * RING + me_y)[:, None, None])
    item = jnp.sum(jnp.where(match, item_at, 0), axis=(1, 2))
    right_at = jnp.sum(jnp.where(match, row_groups[None], 0), axis=(1, 2))
    left_at = (me_z * RING + y_from) * sectors + item // states
    index_table = jnp.stack(
        [
            z_to,
            y_from,
            z_rank,
            y_rank,
            item // states,
            right_at % sectors,
            pick(left_dims, left_at),
            pick(right_dims, right_at),
        ]
    )
    state_at = jnp.arange(states, dtype=jnp.int32)
    weight_table = jnp.sum(
        jnp.where((item % states)[None, :, None] == state_at, site_weights[:, None, :], 0.0), axis=-1
    )
    my_group = me_z * RING + me_y
    my_rights = lax.dynamic_index_in_dim(right_groups, my_group, 0, keepdims=False)
    targets = me_o * RING + jnp.arange(RING, dtype=jnp.int32)
    chosen_match = (my_rights // sectors)[None, :] == targets[:, None]
    chosen = jnp.sum(jnp.where(chosen_match, item_at, 0), axis=1)
    chosen_right = jnp.sum(jnp.where(chosen_match, my_rights[None], 0), axis=1)
    row_end = pick(left_dims, my_group * sectors + chosen // states)
    column_end = pick(right_dims, chosen_right)
    places = jnp.arange(width, dtype=jnp.int32)
    keep = (places[None, :, None] < row_end[:, None, None]) & (
        places[None, None, :] < column_end[:, None, None]
    )
    taken = jnp.take(wavefunction.reshape(items, width, width), chosen, axis=0)
    outgoing = jnp.where(keep, taken, jnp.zeros_like(taken))
    owned = my_group * sectors + jnp.arange(sectors, dtype=jnp.int32)
    sector_at = jnp.arange(groups * sectors, dtype=jnp.int32)
    source = jnp.sum(
        jnp.where(right_sector[None] == owned[:, None, None], sector_at[None, :, None] // sectors, 0),
        axis=1,
    ).reshape(-1)
    slot_table = jnp.stack(
        [pick(rank, (source // RING - me_z) % RING), pick(rank, (me_y - source % RING) % RING)]
    )
    vectors = basis.shape[0]
    sigma, sums = fused(
        index_table,
        weight_table,
        slot_table,
        outgoing,
        left_ops,
        right_ops,
        basis.reshape(vectors, items, -1, width),
    )
    return sigma.reshape(sectors, states, -1, width), jnp.sum(sums[:vectors], axis=1)


def solution(mesh):
    grid = Mesh(mesh.devices.reshape(RING, RING, RING), ("ops", "z", "y"))
    sec = ("z", "y")
    in_specs = (
        P(sec, None, None, None),
        P("ops", sec, None, None),
        P("ops", sec, None, None),
        P("ops", None),
        P(),
        P(),
        P(),
        P(None, sec, None, "ops", None),
    )
    out_specs = (P(sec, None, "ops", None), P())
    return jax.shard_map(
        per_device, mesh=grid, in_specs=in_specs, out_specs=out_specs, check_vma=False
    )
```

time: 374 us -> 125 us (0.33)
  waiting for transfers between devices: 194 us -> 0 us
  blocking collectives: 117 us -> 0 us
  Pallas kernels: 27 us -> 106 us
  between operations: 13.9 us -> 0.78 us
  starting transfers between devices: 6.62 us -> 0 us
    all_gather x3 -> x0, waiting for transfers between devices: 145 us -> none  [the longest x1 59.4 us: per_device(): right_all = lax.all_gather(right_ops, 'z', axis=0)]
    psum x1 -> x0, blocking collectives: 100 us -> none  [per_device(): return (sigma, lax.psum(local, ('ops', 'z', 'y')))]
    pallas_call x1, Pallas kernels: 27 us -> 106 us  [fused(): pl.pallas_call(kernel, out_shape=(jax.ShapeDtypeStruct((pairs, share, wid...]
    reduce_scatter x1 -> x0, waiting for transfers between devices: 38.2 us -> none  [per_device(): lax.psum_scatter(partial, 'ops', scatter_dimension=1, tiled=True)]
    all_to_all x1 -> x0, blocking collectives: 17 us -> none  [per_device(): lax.all_to_all(outgoing, 'y', split_axis=0, concat_axis=0, tiled=True)]
    all_to_all x1 -> x0, waiting for transfers between devices: 9.44 us -> none  [per_device(): lax.all_to_all(summed, 'z', split_axis=0, concat_axis=0, tiled=True)]
    all_to_all x1 -> x0, starting transfers between devices: 6.46 us -> none  [per_device(): lax.all_to_all(summed, 'z', split_axis=0, concat_axis=0, tiled=True)]
    reduce_sum x5 -> x9, other arithmetic: 3.88 us -> 8.27 us  [the longest x5 4.19 us: pick(): return jnp.sum(jnp.where(positions[..., None] == places, table, 0), axis=-1)]
  transfers between devices with their start and end apart: 5 -> 0, of which waited for: 5 -> 0; matrix products, arithmetic and copies ran while one was open for 1% -> 0% of each run, Pallas kernels for 0% -> 0%
where the time goes in v2:
time: 125 us; the launch traced here: 124 us
  Pallas kernels  106 us (85%)
  other arithmetic  11.1 us (9%)
  local copies, waits for them, and re-layouts  6.63 us (5%)
    pallas_call x1, Pallas kernels, fused(): pl.pallas_call(kernel, out_shape=(jax.ShapeDtypeStruct((pairs, share, wid...  106 us
    unnamed x10, local copies, waits for them, and re-layouts  5.16 us
    reduce_sum x5, other arithmetic, pick(): return jnp.sum(jnp.where(positions[..., None] == places, table, 0), axis=-1)  4.19 us
    reduce_sum x1, other arithmetic, per_device(): right_at = jnp.sum(jnp.where(match, row_groups[None], 0), axis=(1, 2))  2.51 us

profile of v2, /device:TPU:1, one launch (start us, length us, event | category | flops | bytes accessed | tf_op | source)
XLA Modules:
  0.0 124.3 jit_solution(2951013922551849162)
XLA Ops:
  0.6 0.0 copy-start
  0.6 0.0 copy-start.1
  0.7 1.6 %copy-done = bf16[4,16,128,128]{3,2,1,0:T(8,128)(2,1)S(1)} copy-done((bf16[4,16,128,128]{3,2,1,0:T(8,128)(2,1)S(1)}, bf16[4,16,128,128]{3,2,1,0:T(8,128)(2,1)}, u32[]{:S(2)}) %copy-start) | copy-done | bytes 2097176
  2.2 0.9 select_reduce_fusion.2
  3.2 0.1 reshape.374
  3.2 0.7 and_select_fusion.3
  3.9 0.7 select_reduce_fusion.9
  4.7 0.7 multiply_add_fusion.1
  5.4 0.1 iota_compare_fusion.2
  5.4 0.8 copy.19
  6.2 0.1 reshape.373
  6.4 2.5 %select_reduce_fusion = (s32[64]{0:T(128)S(1)}, s32[64]{0:T(128)S(1)}) fusion(s32[8,64]{1,0:T(8,128)S(1)} %get-tuple-element.15, s32[8,64]{1,0:T(8,128)S(1)} %get-tuple-element.14, s32[64]{0:T(128)S(1)} %get-tuple-element.12, pred[64,8]{1,0:T(8,128)(4,1)S(1)} %iota_compare_fusion.2), kind=kLoop, calls=%fused_computation.2 | loop fusion | flops 196480 | bytes 5376 | tf_op jit(solution)/shard_map/reduce_sum | solution.py:429
  8.9 0.2 fusion.1
  9.1 0.9 select_reduce_fusion.6
  10.0 0.9 select_reduce_fusion.7
  10.9 0.9 select_reduce_fusion.3
  11.8 0.9 select_reduce_fusion.4
  12.6 0.7 stack.38.index_ref
  13.3 0.1 iota_compare_fusion.6
  13.4 0.8 select_reduce_fusion.5.weight_ref
  14.2 0.6 gather_fusion
  14.8 0.2 and_select_fusion.outgoing_ref
  15.0 0.0 copy-done.1
  15.1 0.0 copy-start.2
  15.1 1.0 copy-done.2
  16.1 0.0 copy-start.3
  16.1 1.0 copy-done.3
  17.1 105.9 %shard_map.140 = (bf16[64,16,128]{2,1,0:T(8,128)(2,1)S(1)}, f32[8,128]{1,0:T(8,128)S(1)}) custom-call(s32[8,64]{1,0:T(8,128)S(1)} %stack.38.index_ref, f32[4,64]{1,0:T(4,128)S(1)} %select_reduce_fusion.5.weight_ref, s32[2,64]{1,0:T(2,128)S(1)} %pad_add_fusion.slot_ref, bf16[8,128,128]{2,1,0:T(8,128)(2,1)S(1)} %and_select_fusion.outgoing_ref, ...), custom_call_target="tpu_custom_call" | custom-call | tf_op jit(solution)/shard_map/pallas_call | solution.py:361
  123.0 0.6 slice_reduce_fusion
  123.6 0.7 copy.21
  (14 shorter events, 0.1 us)
Async XLA Ops:
  0.6 1.6 %copy-start = (bf16[4,16,128,128]{3,2,1,0:T(8,128)(2,1)S(1)}, bf16[4,16,128,128]{3,2,1,0:T(8,128)(2,1)}, u32[]{:S(2)}) copy-start(bf16[4,16,128,128]{3,2,1,0:T(8,128)(2,1)} %param.13) | copy-start | bytes 6291460
  0.6 14.4 %copy-start.1 = (bf16[4,4,16,16,128]{4,3,2,1,0:T(8,128)(2,1)S(1)}, bf16[4,4,16,16,128]{4,3,2,1,0:T(8,128)(2,1)}, u32[]{:S(2)}) copy-start(bf16[4,4,16,16,128]{4,3,2,1,0:T(8,128)(2,1)} %param.20) | copy-start | bytes 3145732
  15.1 1.0 copy-start.2
  16.1 1.0 copy-start.3

commit v3 on v2

v3 whole, which is shorter than its diff:
```python
import jax
import jax.numpy as jnp
from jax import lax
from jax.experimental import pallas as pl
from jax.experimental.pallas import tpu as pltpu
from jax.sharding import Mesh
from jax.sharding import PartitionSpec as P

MESH = pl.DeviceIdType.MESH
RING = 8
CHIPS = 4
DISTANCE = (0, 1, 7, 2, 6, 3, 5, 4)
RANK = tuple(DISTANCE.index(d) for d in range(RING))
READY = (1, 3, 5, 7, 8)


def pair_order():
    order, before = [], 0
    for ready in READY:
        for z_rank in range(ready):
            for y_rank in range(ready):
                if max(z_rank, y_rank) >= before:
                    order.append((z_rank, y_rank))
        before = ready
    return order


ORDER = pair_order()
CHUNKS = ((1, 0, 9), (2, 9, 25), (3, 25, 33), (3, 33, 41), (3, 41, 49), (4, 49, 57), (4, 57, 64))


def kernel(
    order_ref,
    weight_ref,
    left_dim_ref,
    right_dim_ref,
    sector_ref,
    wave_hbm,
    left_ref,
    right_ref,
    basis_hbm,
    sigma_ref,
    sums_ref,
    wave_ref,
    basis_ref,
    outgoing_ref,
    made_ref,
    table_ref,
    slab_ref,
    left_land,
    right_land,
    left_all,
    right_all,
    split_ref,
    pair_ref,
    row_ref,
    chip_ref,
    final_ref,
    arrive_ref,
    tally_ref,
    local_sem,
    fetch_sem,
    slab_send,
    slab_recv,
    spread_send,
    spread_recv,
    mate_send,
    mate_recv,
    ring_send,
    ring_recv,
    pair_send,
    pair_recv,
    chip_send,
    chip_recv,
    final_send,
    final_recv,
    tally_send,
    tally_recv,
):
    me_o, me_z, me_y = lax.axis_index("ops"), lax.axis_index("z"), lax.axis_index("y")
    me_x, core = me_o // 2, me_o % 2
    mate = me_x * 2 + 1 - core
    mine = {"ops": me_o, "z": me_z, "y": me_y}
    terms, width = left_ref.shape[0], left_ref.shape[-1]
    half = terms // 2
    sectors = left_ref.shape[1]
    states = weight_ref.shape[1]
    my_group = me_z * RING + me_y
    started = []

    def device(axis, position):
        return tuple(
            position if name == axis else mine[name] for name in ("ops", "z", "y")
        )

    def send(source, target, send_sem, recv_sem, axis, position):
        copy = pltpu.make_async_remote_copy(
            src_ref=source,
            dst_ref=target,
            send_sem=send_sem,
            recv_sem=recv_sem,
            device_id=device(axis, position),
            device_id_type=MESH,
        )
        copy.start()
        started.append(copy)
        return copy

    def chip_at(step):
        return lax.rem(me_x + step, CHIPS)

    def ring_at(position, step):
        return lax.rem(position + step, RING)

    fetches = [
        pltpu.make_async_copy(source, target, fetch_sem.at[place])
        for place, (source, target) in enumerate(
            (
                (wave_hbm, wave_ref),
                (left_ref, left_land.at[0]),
                (right_ref, right_land.at[0]),
                (basis_hbm, basis_ref),
            )
        )
    ]
    for fetch in fetches:
        fetch.start()

    barrier = pltpu.get_barrier_semaphore()
    for axis in ("ops", "z", "y"):
        for step in range(1, RING):
            pl.semaphore_signal(
                barrier,
                inc=1,
                device_id=device(axis, ring_at(mine[axis], step)),
                device_id_type=MESH,
            )
    pl.semaphore_wait(barrier, 3 * (RING - 1))

    sides = ((left_ref, left_land, "y"), (right_ref, right_land, "z"))
    flying = {}

    def pass_on(stage, part):
        for side, (held, land, axis) in enumerate(sides):
            for way in range(2):
                if stage == 3 and part != way:
                    continue
                here = stage if way == 0 else (RING - stage) % RING
                there = stage + 1 if way == 0 else RING - 1 - stage
                terms_at = pl.ds(part * half, half)
                source = held.at[terms_at] if stage == 0 else land.at[RANK[here], terms_at]
                sem = ((side * 2 + way) * 4 + stage) * 2 + part
                flying[side, way, stage, part] = send(
                    source,
                    land.at[RANK[there], terms_at],
                    ring_send.at[sem],
                    ring_recv.at[sem],
                    axis,
                    ring_at(mine[axis], 1 if way == 0 else RING - 1),
                )

    def take_in(stage, part):
        for side in range(2):
            for way in range(2):
                if stage == 3 and part != way:
                    continue
                flying[side, way, stage, part].wait_recv()

    def keep_block(held, kept, rank):
        def one(term, carry):
            kept[rank, term] = held[term]
            return carry

        lax.fori_loop(0, terms, one, 0)

    rows = lax.broadcasted_iota(jnp.int32, (width, width), 0)
    columns = lax.broadcasted_iota(jnp.int32, (width, width), 1)
    share = width // RING

    def far(rank):
        return jnp.where(rank % 2 == 1, (rank + 1) // 2, (RING - rank // 2) % RING)

    def make_tables():
        lanes = lax.broadcasted_iota(jnp.int32, (RING, width), 1)
        sublanes = lax.broadcasted_iota(jnp.int32, (RING, 1), 0)
        items = sector_ref.shape[1]
        item_at = lax.broadcasted_iota(jnp.int32, (RING, items), 1)

        def find(group, wanted):
            held = jnp.broadcast_to(sector_ref[pl.ds(group, 1), :], (RING, items))
            match = held // sectors == wanted
            return (
                jnp.max(jnp.where(match, item_at, 0), axis=1, keepdims=True),
                jnp.max(jnp.where(match, held, 0), axis=1, keepdims=True),
            )

        made_ref[...] = jnp.zeros(made_ref.shape, jnp.int32)
        z_to = (me_z + RING - far(sublanes)) % RING
        made = jnp.zeros((RING, width), jnp.int32)
        for y_rank in range(RING):
            group = me_z * RING + ring_at(me_y, RING - DISTANCE[y_rank])
            item, right = find(group, z_to * RING + me_y)
            made = jnp.where(lanes == y_rank, item, made)
            made = jnp.where(lanes == RING + y_rank, right, made)
        item, right = find(my_group, me_o * RING + sublanes)
        made = jnp.where(lanes == 2 * RING, item, made)
        made = jnp.where(lanes == 2 * RING + 1, right, made)
        made_ref[pl.ds(0, RING), :] = made
        table = sector_ref[...]
        group_at = lax.broadcasted_iota(jnp.int32, table.shape, 0)
        for sector in range(sectors):
            match = table == my_group * sectors + sector
            made_ref[pl.ds(RING + sector, 1), pl.ds(0, items)] = jnp.max(
                jnp.where(match, group_at, 0), axis=0, keepdims=True
            )
        copy = pltpu.make_async_copy(made_ref, table_ref, fetch_sem.at[4])
        copy.start()
        copy.wait()

    def kept(left_at, right_at):
        return (rows < left_dim_ref[left_at]) & (columns < right_dim_ref[right_at])

    def pick_slabs():
        def one(place, carry):
            item, right = table_ref[place, 2 * RING], table_ref[place, 2 * RING + 1]
            keep = kept(my_group * sectors + item // states, right)
            slab = jnp.where(keep, wave_ref[item].astype(jnp.float32), 0.0)
            outgoing_ref[place] = slab.astype(jnp.bfloat16)
            return carry

        lax.fori_loop(0, RING, one, 0)

    def contract(chunk):
        def one(position, carry):
            z_rank, y_rank = order_ref[0, position], order_ref[1, position]
            z_to = lax.rem(me_z + RING - order_ref[2, position], RING)
            y_from = lax.rem(me_y + RING - order_ref[3, position], RING)
            item, right = table_ref[z_rank, y_rank], table_ref[z_rank, RING + y_rank]
            left_at, right_at = item // states, right % sectors
            state = item % states
            slab = slab_ref[z_to, y_from]
            keep = kept((me_z * RING + y_from) * sectors + left_at, right)
            total = jnp.zeros((width, width), jnp.float32)
            for term in range(terms):
                product = jnp.dot(
                    left_all[y_rank, term, left_at], slab, preferred_element_type=jnp.float32
                )
                summand = jnp.dot(
                    product.astype(jnp.bfloat16),
                    right_all[z_rank, term, right_at],
                    preferred_element_type=jnp.float32,
                )
                total += summand * weight_ref[term, state]
            total = jnp.where(keep, total, 0.0)
            for owner in range(RING):
                split_ref[owner % 2, owner // 2, position] = total[
                    owner * share : (owner + 1) * share
                ]
            return carry

        lax.fori_loop(CHUNKS[chunk][1], CHUNKS[chunk][2], one, 0)

    pair_copies, chip_copies = {}, {}

    def span(chunk):
        return pl.ds(CHUNKS[chunk][1], CHUNKS[chunk][2] - CHUNKS[chunk][1])

    def to_mate(chunk):
        pair_copies[chunk] = send(
            split_ref.at[1 - core, :, span(chunk)],
            pair_ref.at[:, span(chunk)],
            pair_send.at[chunk],
            pair_recv.at[chunk],
            "ops",
            mate,
        )

    def to_chips(chunk):
        pair_copies[chunk].wait_recv()

        def one(position, carry):
            for chip in range(CHIPS):
                row_ref[chip, position] = (
                    split_ref[core, chip, position] + pair_ref[chip, position]
                )
            return carry

        lax.fori_loop(CHUNKS[chunk][1], CHUNKS[chunk][2], one, 0)
        for step in range(1, CHIPS):
            chip_copies[chunk, step] = send(
                row_ref.at[chip_at(step), span(chunk)],
                chip_ref.at[step - 1, span(chunk)],
                chip_send.at[chunk * CHIPS + step],
                chip_recv.at[chunk * CHIPS + step],
                "ops",
                chip_at(step) * 2 + core,
            )

    pass_on(0, 0)
    pass_on(0, 1)
    make_tables()
    fetches[0].wait()
    pick_slabs()
    own = pltpu.make_async_copy(
        outgoing_ref.at[me_y], slab_ref.at[me_o, me_y], local_sem
    )
    own.start()
    slab_copies = [
        send(
            outgoing_ref.at[ring_at(me_y, step)],
            slab_ref.at[me_o, me_y],
            slab_send.at[step],
            slab_recv.at[step],
            "y",
            ring_at(me_y, step),
        )
        for step in range(1, RING)
    ]

    own.wait()
    for copy in slab_copies:
        copy.wait_recv()
    spread = [
        send(
            slab_ref.at[me_o],
            slab_ref.at[me_o],
            spread_send.at[step],
            spread_recv.at[step],
            "ops",
            chip_at(step) * 2 + core,
        )
        for step in range(1, CHIPS)
    ]
    mates = [
        send(slab_ref.at[me_o], slab_ref.at[me_o], mate_send.at[0], mate_recv.at[0], "ops", mate)
    ]
    fetches[1].wait()
    fetches[2].wait()
    keep_block(left_land.at[0], left_all, 0)
    keep_block(right_land.at[0], right_all, 0)
    take_in(0, 0)
    pass_on(1, 0)
    for step in range(1, CHIPS):
        spread[step - 1].wait_recv()
        block = chip_at(CHIPS - step) * 2 + core
        mates.append(
            send(
                slab_ref.at[block],
                slab_ref.at[block],
                mate_send.at[step],
                mate_recv.at[step],
                "ops",
                mate,
            )
        )
    take_in(0, 1)
    pass_on(1, 1)
    for copy in mates:
        copy.wait_recv()

    stage, waiting = 0, []
    for chunk in range(len(CHUNKS)):
        if CHUNKS[chunk][0] != stage:
            stage = CHUNKS[chunk][0]
            if stage > 1:
                for part in range(2):
                    take_in(stage - 1, part)
                    if stage < 4:
                        pass_on(stage, part)
            for rank in range(READY[stage - 1], READY[stage]):
                keep_block(left_land.at[rank], left_all, rank)
                keep_block(right_land.at[rank], right_all, rank)
            if stage < 4:
                while waiting:
                    to_chips(waiting.pop(0))
        contract(chunk)
        to_mate(chunk)
        while waiting:
            to_chips(waiting.pop(0))
        waiting.append(chunk)
    to_chips(waiting.pop(0))
    for chunk in range(len(CHUNKS)):
        for step in range(1, CHIPS):
            chip_copies[chunk, step].wait_recv()

    final_copies = []
    for z_rank in reversed(range(RING)):
        for y_rank in range(RING):
            position = ORDER.index((z_rank, y_rank))
            value = row_ref[me_x, position] + chip_ref[0, position]
            value = value + chip_ref[1, position] + chip_ref[2, position]
            target = final_ref if z_rank else arrive_ref
            target[z_rank, y_rank] = value.astype(jnp.bfloat16)
        if z_rank:
            final_copies.append(
                send(
                    final_ref.at[z_rank],
                    arrive_ref.at[z_rank],
                    final_send.at[z_rank],
                    final_recv.at[z_rank],
                    "z",
                    ring_at(me_z, RING - DISTANCE[z_rank]),
                )
            )
    for copy in final_copies:
        copy.wait_recv()

    vectors = basis_ref.shape[0]
    fetches[3].wait()

    def near(distance):
        back = jnp.where(distance == 0, 0, 2 * (RING - distance))
        return jnp.where((distance > 0) & (distance <= RING // 2), 2 * distance - 1, back)

    def project(item, sums):
        sector, state = item // states, item % states
        source = table_ref[RING + sector, state]
        for step in range(1, sectors):
            source = jnp.maximum(source, table_ref[RING + sector, step * states + state])
        z_rank = near(lax.rem(source // RING + RING - me_z, RING))
        y_rank = near(lax.rem(me_y + RING - source % RING, RING))
        value = arrive_ref[z_rank, y_rank]
        sigma_ref[item] = value
        wide = value.astype(jnp.float32)
        return tuple(
            sums[vector] + basis_ref[vector, item].astype(jnp.float32) * wide
            for vector in range(vectors)
        )

    zero = jnp.zeros((share, width), jnp.float32)
    sums = lax.fori_loop(0, basis_ref.shape[1], project, (zero,) * vectors)
    now = jnp.concatenate([jnp.sum(value, axis=0, keepdims=True) for value in sums] * 2, axis=0)

    for phase, axis in enumerate(("ops", "z", "y")):
        tally_ref[phase, mine[axis]] = now
        copies = [
            send(
                tally_ref.at[phase, mine[axis]],
                tally_ref.at[phase, mine[axis]],
                tally_send.at[phase * RING + step],
                tally_recv.at[phase * RING + step],
                axis,
                ring_at(mine[axis], step),
            )
            for step in range(1, RING)
        ]
        for copy in copies:
            copy.wait_recv()
        now = tally_ref[phase, 0]
        for other in range(1, RING):
            now = now + tally_ref[phase, other]
    sums_ref[...] = now
    for copy in started:
        copy.wait_send()


def fused(order, site_weights, left_dims, right_dims, sector_table, wave, left_ops, right_ops, basis):
    smem = pl.BlockSpec(memory_space=pltpu.SMEM)
    vmem = pl.BlockSpec(memory_space=pltpu.VMEM)
    hbm = pl.BlockSpec(memory_space=pl.ANY)
    terms, sectors, width, _ = left_ops.shape
    pairs = RING * RING
    share = width // RING
    block = (RING, terms, sectors, width, width)
    dma = pltpu.SemaphoreType.DMA
    bf16, f32, i32 = jnp.bfloat16, jnp.float32, jnp.int32
    chunks = len(CHUNKS)
    return pl.pallas_call(
        kernel,
        out_shape=(
            jax.ShapeDtypeStruct((pairs, share, width), bf16),
            jax.ShapeDtypeStruct((2 * basis.shape[0], width), f32),
        ),
        in_specs=[smem] * 4 + [vmem] + [hbm] * 4,
        out_specs=(vmem, vmem),
        scratch_shapes=[
            pltpu.VMEM(wave.shape, bf16),
            pltpu.VMEM(basis.shape, bf16),
            pltpu.VMEM((RING, width, width), bf16),
            pltpu.VMEM((2 * RING, width), i32),
            pltpu.SMEM((2 * RING, width), i32),
            pltpu.VMEM((RING, RING, width, width), bf16),
            pltpu.VMEM(block, bf16),
            pltpu.VMEM(block, bf16),
            pltpu.VMEM(block, bf16),
            pltpu.VMEM(block, bf16),
            pltpu.VMEM((2, CHIPS, pairs, share, width), f32),
            pltpu.VMEM((CHIPS, pairs, share, width), f32),
            pltpu.VMEM((CHIPS, pairs, share, width), f32),
            pltpu.VMEM((CHIPS - 1, pairs, share, width), f32),
            pltpu.VMEM((RING, RING, share, width), bf16),
            pltpu.VMEM((RING, RING, share, width), bf16),
            pltpu.VMEM((3, RING, 2 * basis.shape[0], width), f32),
            dma,
            dma((5,)),
            dma((RING,)),
            dma((RING,)),
            dma((CHIPS,)),
            dma((CHIPS,)),
            dma((CHIPS,)),
            dma((CHIPS,)),
            dma((32,)),
            dma((32,)),
            dma((chunks,)),
            dma((chunks,)),
            dma((chunks * CHIPS,)),
            dma((chunks * CHIPS,)),
            dma((RING,)),
            dma((RING,)),
            dma((3 * RING,)),
            dma((3 * RING,)),
        ],
        compiler_params=pltpu.CompilerParams(
            collective_id=0, has_side_effects=True, vmem_limit_bytes=52 << 20
        ),
    )(order, site_weights, left_dims, right_dims, sector_table, wave, left_ops, right_ops, basis)


def per_device(
    wavefunction, left_ops, right_ops, site_weights, right_sector, left_dims, right_dims, basis
):
    sectors, states, width, _ = wavefunction.shape
    items = sectors * states
    vectors = basis.shape[0]
    order = jnp.array(
        [
            [pair[0] for pair in ORDER],
            [pair[1] for pair in ORDER],
            [DISTANCE[pair[0]] for pair in ORDER],
            [DISTANCE[pair[1]] for pair in ORDER],
        ],
        jnp.int32,
    )
    sigma, sums = fused(
        order,
        site_weights,
        left_dims,
        right_dims,
        right_sector.reshape(RING * RING, items),
        wavefunction.reshape(items, width, width),
        left_ops,
        right_ops,
        basis.reshape(vectors, items, -1, width),
    )
    return sigma.reshape(sectors, states, -1, width), jnp.sum(sums[:vectors], axis=1)


def solution(mesh):
    grid = Mesh(mesh.devices.reshape(RING, RING, RING), ("ops", "z", "y"))
    sec = ("z", "y")
    in_specs = (
        P(sec, None, None, None),
        P("ops", sec, None, None),
        P("ops", sec, None, None),
        P("ops", None),
        P(),
        P(),
        P(),
        P(None, sec, None, "ops", None),
    )
    out_specs = (P(sec, None, "ops", None), P())
    return jax.shard_map(
        per_device, mesh=grid, in_specs=in_specs, out_specs=out_specs, check_vma=False
    )
```

time: 125 us -> 119 us (0.952)
  other arithmetic: 11.1 us -> 0.62 us
  Pallas kernels: 106 us -> 111 us
    reduce_sum x9 -> x0, other arithmetic: 8.58 us -> none  [the longest x5 4.19 us: pick(): return jnp.sum(jnp.where(positions[..., None] == places, table, 0), axis=-1)]
    pallas_call x1, Pallas kernels: 106 us -> 111 us  [fused(): pl.pallas_call(kernel, out_shape=(jax.ShapeDtypeStruct((pairs, share, wid...]
    unnamed x10 -> x14, local copies, waits for them, and re-layouts: 5.16 us -> 6.32 us
where the time goes in v3:
time: 119 us
  Pallas kernels  111 us (93%)
  local copies, waits for them, and re-layouts  6.4 us (5%)
    pallas_call x1, Pallas kernels, fused(): pl.pallas_call(kernel, out_shape=(jax.ShapeDtypeStruct((pairs, share, wid...  111 us
    unnamed x14, local copies, waits for them, and re-layouts  6.32 us

profile of v3, /device:TPU:1, one launch (start us, length us, event | category | flops | bytes accessed | tf_op | source)
XLA Modules:
  0.0 118.7 jit_solution(12452725820609077120)
XLA Ops:
  0.6 0.8 copy.12
  1.4 0.1 reshape.16.sector_ref
  1.5 0.0 copy-start
  1.6 1.0 copy-done
  2.6 0.0 copy-start.1
  2.6 1.0 copy-done.1
  3.6 0.0 copy-start.2
  3.6 0.7 copy-done.2
  4.3 0.0 copy-start.3
  4.3 0.7 copy-done.3
  5.0 0.0 copy-start.4
  5.0 0.7 copy-done.4
  5.7 0.0 copy-start.5
  5.7 0.7 copy-done.5
  6.4 111.0 %shard_map.104 = (bf16[64,16,128]{2,1,0:T(8,128)(2,1)S(1)}, f32[8,128]{1,0:T(8,128)S(1)}) custom-call(s32[4,64]{1,0:T(4,128)S(1)} %copy-done.3, f32[4,16]{1,0:T(4,128)S(1)} %copy-done.2, s32[256]{0:T(256)S(1)} %copy-done.4, s32[256]{0:T(256)S(1)} %copy-done.5, s32[64,64]{1,0:T(8,128)S(1)} %reshape.16.sector_ref, bf16[64,128,128]{2,1,0:T(8,128)(2,1)} %bitcast.4, ...), custom_call_target="tpu_custom_call" | custom-call | tf_op jit(solution)/shard_map/pallas_call | solution.py:468
  117.4 0.6 slice_reduce_fusion
  118.0 0.7 copy.14
Async XLA Ops:
  1.5 1.0 copy-start
  2.6 1.0 copy-start.1
  3.6 0.7 copy-start.2
  4.3 0.7 copy-start.3
  5.0 0.7 copy-start.4
  5.7 0.7 copy-start.5

commit v4 on v3

--- a/solution.py
+++ b/solution.py
@@ -54,6 +54,7 @@
     split_ref,
     pair_ref,
     row_ref,
+    relay_ref,
     chip_ref,
     final_ref,
     arrive_ref,
@@ -72,6 +73,8 @@
     pair_recv,
     chip_send,
     chip_recv,
+    near_send,
+    near_recv,
     final_send,
     final_recv,
     tally_send,
@@ -260,7 +263,16 @@
 
         lax.fori_loop(CHUNKS[chunk][1], CHUNKS[chunk][2], one, 0)
 
-    pair_copies, chip_copies = {}, {}
+    pair_copies, chip_copies, near_copies = {}, {}, {}
+
+    def part_ends(chunk, way):
+        _, first, end = CHUNKS[chunk]
+        middle = (first + end) // 2
+        return (first, middle) if way == 0 else (middle, end)
+
+    def part_span(chunk, way):
+        first, end = part_ends(chunk, way)
+        return pl.ds(first, end - first)
 
     def span(chunk):
         return pl.ds(CHUNKS[chunk][1], CHUNKS[chunk][2] - CHUNKS[chunk][1])
@@ -286,18 +298,37 @@
             return carry
 
         lax.fori_loop(CHUNKS[chunk][1], CHUNKS[chunk][2], one, 0)
-        for step in range(1, CHIPS):
-            chip_copies[chunk, step] = send(
-                row_ref.at[chip_at(step), span(chunk)],
-                chip_ref.at[step - 1, span(chunk)],
-                chip_send.at[chunk * CHIPS + step],
-                chip_recv.at[chunk * CHIPS + step],
+        for way in range(2):
+            chip_copies[chunk, way] = send(
+                row_ref.at[chip_at(2), part_span(chunk, way)],
+                relay_ref.at[part_span(chunk, way)],
+                chip_send.at[chunk * 2 + way],
+                chip_recv.at[chunk * 2 + way],
                 "ops",
-                chip_at(step) * 2 + core,
+                chip_at(1 if way == 0 else CHIPS - 1) * 2 + core,
+            )
+
+    def to_near(chunk):
+        for way in range(2):
+            chip_copies[chunk, way].wait_recv()
+            target = chip_at(1 if way == 0 else CHIPS - 1)
+            first, end = part_ends(chunk, way)
+
+            def one(position, carry):
+                row_ref[target, position] = row_ref[target, position] + relay_ref[position]
+                return carry
+
+            lax.fori_loop(first, end, one, 0)
+            near_copies[chunk, way] = send(
+                row_ref.at[target, span(chunk)],
+                chip_ref.at[way, span(chunk)],
+                near_send.at[chunk * 2 + way],
+                near_recv.at[chunk * 2 + way],
+                "ops",
+                target * 2 + core,
             )
 
     pass_on(0, 0)
-    pass_on(0, 1)
     make_tables()
     fetches[0].wait()
     pick_slabs()
@@ -317,6 +348,9 @@
         for step in range(1, RING)
     ]
 
+    pass_on(0, 1)
+    take_in(0, 0)
+    pass_on(1, 0)
     own.wait()
     for copy in slab_copies:
         copy.wait_recv()
@@ -338,8 +372,11 @@
     fetches[2].wait()
     keep_block(left_land.at[0], left_all, 0)
     keep_block(right_land.at[0], right_all, 0)
-    take_in(0, 0)
-    pass_on(1, 0)
+    take_in(0, 1)
+    pass_on(1, 1)
+    for rank in range(1, READY[1]):
+        keep_block(left_land.at[rank], left_all, rank)
+        keep_block(right_land.at[rank], right_all, rank)
     for step in range(1, CHIPS):
         spread[step - 1].wait_recv()
         block = chip_at(CHIPS - step) * 2 + core
@@ -353,42 +390,43 @@
                 mate,
             )
         )
-    take_in(0, 1)
-    pass_on(1, 1)
+    take_in(1, 0)
+    pass_on(2, 0)
     for copy in mates:
         copy.wait_recv()
 
-    stage, waiting = 0, []
+    stage, to_split, to_add = 1, [], []
     for chunk in range(len(CHUNKS)):
         if CHUNKS[chunk][0] != stage:
             stage = CHUNKS[chunk][0]
-            if stage > 1:
-                for part in range(2):
-                    take_in(stage - 1, part)
-                    if stage < 4:
-                        pass_on(stage, part)
+            for part in range(1 if stage == 2 else 0, 2):
+                take_in(stage - 1, part)
+                if stage < 4:
+                    pass_on(stage, part)
             for rank in range(READY[stage - 1], READY[stage]):
                 keep_block(left_land.at[rank], left_all, rank)
                 keep_block(right_land.at[rank], right_all, rank)
-            if stage < 4:
-                while waiting:
-                    to_chips(waiting.pop(0))
         contract(chunk)
         to_mate(chunk)
-        while waiting:
-            to_chips(waiting.pop(0))
-        waiting.append(chunk)
-    to_chips(waiting.pop(0))
+        if to_add:
+            to_near(to_add.pop(0))
+        if to_split:
+            to_add.append(to_split.pop(0))
+            to_chips(to_add[-1])
+        to_split.append(chunk)
+    to_add.append(to_split.pop(0))
+    to_chips(to_add[-1])
+    while to_add:
+        to_near(to_add.pop(0))
     for chunk in range(len(CHUNKS)):
-        for step in range(1, CHIPS):
-            chip_copies[chunk, step].wait_recv()
+        for way in range(2):
+            near_copies[chunk, way].wait_recv()
 
     final_copies = []
     for z_rank in reversed(range(RING)):
         for y_rank in range(RING):
             position = ORDER.index((z_rank, y_rank))
-            value = row_ref[me_x, position] + chip_ref[0, position]
-            value = value + chip_ref[1, position] + chip_ref[2, position]
+            value = row_ref[me_x, position] + chip_ref[0, position] + chip_ref[1, position]
             target = final_ref if z_rank else arrive_ref
             target[z_rank, y_rank] = value.astype(jnp.bfloat16)
         if z_rank:
@@ -487,7 +525,8 @@
             pltpu.VMEM((2, CHIPS, pairs, share, width), f32),
             pltpu.VMEM((CHIPS, pairs, share, width), f32),
             pltpu.VMEM((CHIPS, pairs, share, width), f32),
-            pltpu.VMEM((CHIPS - 1, pairs, share, width), f32),
+            pltpu.VMEM((pairs, share, width), f32),
+            pltpu.VMEM((2, pairs, share, width), f32),
             pltpu.VMEM((RING, RING, share, width), bf16),
             pltpu.VMEM((RING, RING, share, width), bf16),
             pltpu.VMEM((3, RING, 2 * basis.shape[0], width), f32),
@@ -503,15 +542,17 @@
             dma((32,)),
             dma((chunks,)),
             dma((chunks,)),
-            dma((chunks * CHIPS,)),
-            dma((chunks * CHIPS,)),
+            dma((chunks * 2,)),
+            dma((chunks * 2,)),
+            dma((chunks * 2,)),
+            dma((chunks * 2,)),
             dma((RING,)),
             dma((RING,)),
             dma((3 * RING,)),
             dma((3 * RING,)),
         ],
         compiler_params=pltpu.CompilerParams(
-            collective_id=0, has_side_effects=True, vmem_limit_bytes=52 << 20
+            collective_id=0, has_side_effects=True, vmem_limit_bytes=67043328
         ),
     )(order, site_weights, left_dims, right_dims, sector_table, wave, left_ops, right_ops, basis)
 

time: 119 us -> 118 us (level)
  local copies, waits for them, and re-layouts: 6.4 us -> 3.19 us
    unnamed x14 -> x2, local copies, waits for them, and re-layouts: 6.32 us -> 2.49 us
where the time goes in v4:
time: 118 us; the launch traced here: 117 us
  Pallas kernels  112 us (95%)
  local copies, waits for them, and re-layouts  3.19 us (3%)
  other arithmetic  1.3 us (1%)
    pallas_call x1, Pallas kernels, fused(): pl.pallas_call(kernel, out_shape=(jax.ShapeDtypeStruct((pairs, share, wid...  112 us
    unnamed x2, local copies, waits for them, and re-layouts  2.49 us

profile of v4, /device:TPU:1, one launch (start us, length us, event | category | flops | bytes accessed | tf_op | source)
XLA Modules:
  0.0 117.3 jit_solution(9355370150739023603)
XLA Ops:
  0.6 0.8 copy.12
  1.4 0.7 reshape.16.sector_ref
  2.2 112.2 %shard_map.104 = (bf16[64,16,128]{2,1,0:T(8,128)(2,1)}, f32[8,128]{1,0:T(8,128)}) custom-call(s32[4,64]{1,0:T(4,128)} %constant.4.clone.order_ref, f32[4,16]{1,0:T(4,128)} %weight_ref.1, s32[256]{0:T(256)} %left_dim_ref.1, s32[256]{0:T(256)} %right_dim_ref.1, s32[64,64]{1,0:T(8,128)} %reshape.16.sector_ref, bf16[64,128,128]{2,1,0:T(8,128)(2,1)} %bitcast.3, ...), custom_call_target="tpu_custom_call" | custom-call | tf_op jit(solution)/shard_map/pallas_call | solution.py:506
  114.4 1.3 %slice_reduce_fusion = f32[4]{0:T(128)} fusion(f32[8,128]{1,0:T(8,128)} %get-tuple-element.5), kind=kLoop, calls=%fused_computation | loop fusion | flops 508 | bytes 2064 | tf_op jit(solution)/shard_map/reduce_sum | solution.py:586
  115.7 1.7 %copy.14 = bf16[4,16,16,128]{3,2,1,0:T(8,128)(2,1)} copy(bf16[4,16,16,128]{3,2,1,0:T(8,128)(2,1)} %bitcast.5) | data formatting | bytes 524288
